TPU v7x, 512 devices: a whole 4x8x8 slice. The times are simulated.
512 devices in a mesh: dp: 64 (over z, y), own: 8 (over x, core).
Axes of the slice: x: 4, y: 8, z: 8, core: 2. Of those that a mesh axis runs over, the one named last changes fastest.
Arguments:
- partial_grads: bfloat16 [64, 112, 16, 4096], P('dp', None, 'own'), may hold values from -1 to 1
- owner_group: int32 [112], replicated, may hold values from 0 to 63, as said below
- master: float32 [128, 16, 4096], P('dp', 'own'), may hold values from -12 to 12
- moment_one: float32 [128, 16, 4096], P('dp', 'own'), may hold values from -3 to 3
- moment_two: float32 [128, 16, 4096], P('dp', 'own'), may hold values from 0.01 to 1
- vec_grads: bfloat16 [64, 64, 4096], P('dp', None, 'own'), may hold values from -1 to 1
- vec_master: float32 [64, 4096], P(None, 'own'), may hold values from 0.5 to 1.5
- vec_first: float32 [64, 4096], P(None, 'own'), may hold values from -3 to 3
- vec_second: float32 [64, 4096], P(None, 'own'), may hold values from 0.01 to 1
Outputs:
- new_master: float32 [128, 16, 4096], P('dp', 'own')
- new_first: float32 [128, 16, 4096], P('dp', 'own')
- new_second: float32 [128, 16, 4096], P('dp', 'own')
- weights: bfloat16 [112, 16, 4096], P(None, 'own')
- new_vec_master: float32 [64, 4096], P(None, 'own')
- new_vec_first: float32 [64, 4096], P(None, 'own')
- new_vec_second: float32 [64, 4096], P(None, 'own')
Inputs may be any that keep to these rules, and one draw needn't show every extreme that they name: `owner_group`: each owner group is named by at most 2 matrices, and some group by exactly 2.
All inputs are finite; a program needn't handle non-finite values.
Results may differ from a plain program's by a relative error of at most 0.001.
Values may be sent and summed in bfloat16 or wider, within the bound.
No kernel may reach another device: no remote copies, remote signals or barrier semaphores. Data moves between devices by JAX's collectives and lax.ppermute only.
A program may use at most 64 MiB of HBM per device.

v0:
```python
import jax
import jax.numpy as jnp
from jax import lax
from jax.sharding import PartitionSpec as P

beta_one = 0.9
beta_two = 0.95
fix_one = 1.0 - 0.9**10
fix_two = 1.0 - 0.95**10
epsilon = 1e-06
decay_rate = 0.1
learn_rate = 0.05


def slot_numbers(owner_group, capacity):
    count = owner_group.shape[0]
    places = jnp.arange(count, dtype=jnp.int32)
    same = owner_group[:, None] == owner_group[None, :]
    before = places[None, :] < places[:, None]
    ranks = jnp.sum((same & before).astype(jnp.int32), axis=1)
    return owner_group * capacity + ranks


def body(
    partial_grads,
    owner_group,
    master,
    moment_one,
    moment_two,
    vec_grads,
    vec_master,
    vec_first,
    vec_second,
):
    groups = lax.axis_size("dp")
    capacity = master.shape[0]
    slot_count = groups * capacity
    slots = slot_numbers(owner_group, capacity)
    matches = slots[None, :] == jnp.arange(slot_count, dtype=jnp.int32)[:, None]
    source = jnp.sum(
        matches.astype(jnp.int32) * jnp.arange(owner_group.shape[0], dtype=jnp.int32)[None, :],
        axis=1,
    )
    occupied = jnp.any(matches, axis=1)
    weight_sq = jnp.sum(master * master, axis=(1, 2))
    sectioned = jnp.take(partial_grads[0], source, axis=0)
    sectioned = jnp.where(occupied[:, None, None], sectioned, jnp.zeros_like(sectioned))
    gradient = lax.psum_scatter(
        sectioned.astype(jnp.float32), "dp", scatter_dimension=0, tiled=True
    )
    my_group = lax.axis_index("dp")
    mine = lax.dynamic_slice_in_dim(occupied, my_group * capacity, capacity)[:, None, None]
    first_raw = beta_one * moment_one + (1.0 - beta_one) * gradient
    second_raw = beta_two * moment_two + (1.0 - beta_two) * gradient * gradient
    update = first_raw / fix_one / (jnp.sqrt(second_raw / fix_two) + epsilon) + decay_rate * master
    update_sq = jnp.sum(update * update, axis=(1, 2))
    weight_total, update_total = lax.psum((weight_sq, update_sq), "own")
    ratio = jnp.sqrt(weight_total) / jnp.sqrt(update_total)
    stepped = master - learn_rate * ratio[:, None, None] * update
    zeros_block = jnp.zeros_like(master)
    new_master = jnp.where(mine, stepped, zeros_block)
    new_first = jnp.where(mine, first_raw, zeros_block)
    new_second = jnp.where(mine, second_raw, zeros_block)
    published = lax.all_gather(new_master.astype(jnp.bfloat16), "dp", axis=0, tiled=True)
    weights = jnp.take(published, slots, axis=0)
    vec_gradient = lax.psum(vec_grads[0].astype(jnp.float32), "dp")
    new_vec_first = beta_one * vec_first + (1.0 - beta_one) * vec_gradient
    new_vec_second = beta_two * vec_second + (1.0 - beta_two) * vec_gradient * vec_gradient
    new_vec_master = vec_master - learn_rate * (new_vec_first / fix_one) / (
        jnp.sqrt(new_vec_second / fix_two) + epsilon
    )
    return (
        new_master,
        new_first,
        new_second,
        weights,
        new_vec_master,
        new_vec_first,
        new_vec_second,
    )


def solution(mesh):
    placed = (
        P("dp", None, "own", None),
        P(),
        P("dp", "own", None),
        P("dp", "own", None),
        P("dp", "own", None),
        P("dp", None, "own"),
        P(None, "own"),
        P(None, "own"),
        P(None, "own"),
    )
    return jax.shard_map(
        body,
        mesh=mesh,
        in_specs=placed,
        out_specs=(
            P("dp", "own", None),
            P("dp", "own", None),
            P("dp", "own", None),
            P(None, "own", None),
            P(None, "own"),
            P(None, "own"),
            P(None, "own"),
        ),
        check_vma=False,
    )
```

profile of v0, /device:TPU:2, one launch (start us, length us, event | category | flops | bytes accessed | tf_op | source)
XLA Modules:
  0.0 314.6 jit_solution(13815475503733527499)
XLA Ops:
  7.2 0.0 copy-start
  7.2 0.0 all-reduce.5.cloned.1.call-start
  7.2 1.0 convert_reduce_fusion
  8.2 0.7 compare_and_fusion
  8.9 0.1 select_reduce_fusion
  9.0 0.1 fusion.3
  9.1 1.5 bitcast_convert_fusion
  10.6 8.0 %gather_fusion = bf16[128,2,4096]{2,1,0:T(2,128)(2,1)} fusion(bf16[112,2,4096]{2,1,0:T(2,128)(2,1)S(1)} %bitcast.9, s32[1024]{0:T(1024)S(1)} %pad_clamp_fusion.1), kind=kCustom, calls=%fused_computation | custom fusion | bytes 4194816 | tf_op jit(solution)/shard_map/jit(_take)/gather | solution.py:46
  18.6 5.7 %fusion = f32[128,2,4096]{2,1,0:T(2,128)} fusion(pred[128]{0:T(512)(128)(4,1)S(1)} %fusion.3, bf16[128,2,4096]{2,1,0:T(2,128)(2,1)} %gather_fusion, pred[128]{0:T(512)(128)(4,1)S(1)} %compare_and_fusion.1), kind=kLoop, calls=%fused_computation.5 | loop fusion | flops 3145728 | bytes 6291712 | tf_op jit(solution)/shard_map/convert_element_type | solution.py:49
  24.4 0.0 copy-start.3
  24.4 0.0 copy-start.4
  24.4 0.0 all-reduce.5.cloned.1.call-update
  24.5 0.0 all-gather.2.cloned.1.call-start
  24.5 0.1 dynamic_slice.3
  24.6 1.3 dynamic-slice
  26.6 173.7 %all-reduce.5.cloned.1.call-done = (f32[128,2,4096]{2,1,0:T(2,128)}, f32[64,512]{1,0:T(8,128)}) async-done(((f32[128,2,4096]{2,1,0:T(2,128)}, f32[64,512]{1,0:T(8,128)}), (f32[128,2,4096]{2,1,0:T(2,128)}, f32[64,512]{1,0:T(8,128)})) %all-reduce.5.cloned.1.call-update) | async-done | bytes 4325392
  200.3 1.9 multiply_reduce_fusion
  202.2 10.0 %all-reduce.2 = (f32[2]{0:T(128)S(1)}, f32[2]{0:T(128)S(1)}) all-reduce(f32[2]{0:T(128)S(1)} %get-tuple-element.18, f32[2]{0:T(128)S(1)} %get-tuple-element.22), channel_id=1, replica_groups=mesh['dp'=64,'own'=8] {'own'}, use_global_device_ids=true, to_apply=%region_7.8 | all-reduce | flops 4 | bytes 32 | tf_op jit(solution)/shard_map/psum | solution.py:57
  212.2 0.8 fusion.7
  212.9 0.0 all-gather.2.cloned.1.call-update
  213.0 1.7 divide_subtract_fusion
  214.7 79.1 %all-gather.2.cloned.1.call-done = bf16[128,2,4096]{2,1,0:T(2,128)(2,1)} async-done(((bf16[2,2,4096]{2,1,0:T(2,128)(2,1)}), bf16[128,2,4096]{2,1,0:T(2,128)(2,1)}) %all-gather.2.cloned.1.call-update) | async-done | bytes 2097168 | tf_op jit(solution)/shard_map/all_gather | solution.py:64
  293.8 9.5 %gather_fusion.1 = bf16[112,2,4096]{2,1,0:T(2,128)(2,1)} fusion(bf16[128,2,4096]{2,1,0:T(2,128)(2,1)} %all-gather.2.cloned.1.call-done, s32[1024]{0:T(1024)S(1)} %pad_clamp_fusion), kind=kCustom, calls=%fused_computation.1 | custom fusion | bytes 3670464 | tf_op jit(solution)/shard_map/jit(_take)/gather | solution.py:65
  303.3 4.5 %broadcast_select_fusion.2 = bf16[112,2,4096]{2,1,0:T(2,128)(2,1)} fusion(bf16[112,2,4096]{2,1,0:T(2,128)(2,1)} %gather_fusion.1, pred[112]{0:T(512)(128)(4,1)S(1)} %get-tuple-element.14), kind=kLoop, calls=%fused_computation.4 | loop fusion | flops 917504 | bytes 3670128 | tf_op jit(solution)/shard_map/jit(_take)/select_n | solution.py:65
  (17 shorter events, 0.1 us)
Async XLA Ops:
  7.2 3.5 %copy-start = (bf16[1,112,2,4096]{3,2,1,0:T(2,128)(2,1)S(1)}, bf16[1,112,2,4096]{3,2,1,0:T(2,128)(2,1)}, u32[]{:S(2)}) copy-start(bf16[1,112,2,4096]{3,2,1,0:T(2,128)(2,1)} %param.9) | copy-start | bytes 5505028
  7.2 193.1 %all-reduce.5.cloned.1.call-start = ((), (), s32[]{:S(2)}) async-start(), calls=%async_computation.1 | async-start | bytes 8650752
  24.4 175.9 %copy-start.1 = (f32[2,2,4096]{2,1,0:T(2,128)S(1)}, f32[2,2,4096]{2,1,0:T(2,128)}, u32[]{:S(2)}) copy-start(f32[2,2,4096]{2,1,0:T(2,128)} %param.11) | copy-start | bytes 196612
  24.4 175.9 %copy-start.5 = (f32[2,2,4096]{2,1,0:T(2,128)S(1)}, f32[2,2,4096]{2,1,0:T(2,128)}, u32[]{:S(2)}) copy-start(f32[2,2,4096]{2,1,0:T(2,128)} %param.13) | copy-start | bytes 196612
  24.4 175.9 %copy-start.6 = (f32[2,2,4096]{2,1,0:T(2,128)S(1)}, f32[2,2,4096]{2,1,0:T(2,128)}, u32[]{:S(2)}) copy-start(f32[2,2,4096]{2,1,0:T(2,128)} %param.12) | copy-start | bytes 196612
  24.4 188.6 %copy-start.2 = (f32[64,512]{1,0:T(8,128)S(1)}, f32[64,512]{1,0:T(8,128)}, u32[]{:S(2)}) copy-start(f32[64,512]{1,0:T(8,128)} %param.15) | copy-start | bytes 393220
  24.4 188.6 %copy-start.3 = (f32[64,512]{1,0:T(8,128)S(1)}, f32[64,512]{1,0:T(8,128)}, u32[]{:S(2)}) copy-start(f32[64,512]{1,0:T(8,128)} %param.16) | copy-start | bytes 393220
  24.4 188.6 %copy-start.4 = (f32[64,512]{1,0:T(8,128)S(1)}, f32[64,512]{1,0:T(8,128)}, u32[]{:S(2)}) copy-start(f32[64,512]{1,0:T(8,128)} %param.17) | copy-start | bytes 393220
  24.5 269.3 %all-gather.2.cloned.1.call-start = ((), (), s32[]{:S(2)}) async-start(), calls=%async_computation | async-start | bytes 2129920 | tf_op jit(solution)/shard_map/all_gather | solution.py:64
Sparse Core Ops, SparseCore 0:
  24.6 175.6 all-reduce.4
  213.1 80.6 all-gather.1
where the time goes:
time: 315 us
  waiting for transfers between devices  253 us (80%)
  local copies, waits for them, and re-layouts  19 us (6%)
  other arithmetic  18 us (6%)
  between operations  14.8 us (5%)
  blocking collectives  9.99 us (3%)
    unnamed x3, waiting for transfers between devices  174 us
    all_gather x1, waiting for transfers between devices, body(): lax.all_gather(new_master.astype(jnp.bfloat16), 'dp', axis=0, tiled=True)  79.1 us
    psum x1, blocking collectives, body(): weight_total, update_total = lax.psum((weight_sq, update_sq), 'own')  9.99 us
    gather x1, local copies, waits for them, and re-layouts, body(): weights = jnp.take(published, slots, axis=0)  9.48 us
    gather x1, local copies, waits for them, and re-layouts, body(): sectioned = jnp.take(partial_grads[0], source, axis=0)  8.02 us
  transfers between devices with their start and end apart: 2, of which 2 were waited for; matrix products, arithmetic and copies ran while one was open for 1% of the time, Pallas kernels for 0%

commit v1 on v0

--- a/solution.py
+++ b/solution.py
@@ -61,7 +61,14 @@
     new_master = jnp.where(mine, stepped, zeros_block)
     new_first = jnp.where(mine, first_raw, zeros_block)
     new_second = jnp.where(mine, second_raw, zeros_block)
-    published = lax.all_gather(new_master.astype(jnp.bfloat16), "dp", axis=0, tiled=True)
+    x_local = new_master.astype(jnp.bfloat16)
+    state_next = jax.lax.all_to_all(
+        jnp.stack([x_local for _ in range(jax.lax.axis_size("dp"))]),
+        "dp",
+        split_axis=0,
+        concat_axis=0,
+    )
+    published = jnp.concatenate(state_next, axis=0)
     weights = jnp.take(published, slots, axis=0)
     vec_gradient = lax.psum(vec_grads[0].astype(jnp.float32), "dp")
     new_vec_first = beta_one * vec_first + (1.0 - beta_one) * vec_gradient

time: 315 us -> 302 us (0.959)
  the two profiles are of different devices: /device:TPU:2 before, /device:TPU:8 now
where the time goes in v1:
time: 302 us
  waiting for transfers between devices  226 us (75%)
  local copies, waits for them, and re-layouts  22.3 us (7%)
  other arithmetic  17.1 us (6%)
  between operations  14.8 us (5%)
  blocking collectives  12.4 us (4%)
  starting transfers between devices  9.46 us (3%)
    unnamed x2, waiting for transfers between devices  174 us
    all_to_all x1, waiting for transfers between devices, body(): jax.lax.all_to_all(jnp.stack([x_local for _ in range(jax.lax.axis_size('d...  52.1 us
    psum x1, blocking collectives, body(): weight_total, update_total = lax.psum((weight_sq, update_sq), 'own')  12.4 us
    gather x1, local copies, waits for them, and re-layouts, body(): weights = jnp.take(published, slots, axis=0)  9.48 us
    all_to_all x1, starting transfers between devices, body(): jax.lax.all_to_all(jnp.stack([x_local for _ in range(jax.lax.axis_size('d...  9.42 us
    gather x1, local copies, waits for them, and re-layouts, body(): sectioned = jnp.take(partial_grads[0], source, axis=0)  8.02 us
  transfers between devices with their start and end apart: 2, of which 2 were waited for; matrix products, arithmetic and copies ran while one was open for 1% of the time, Pallas kernels for 0%

profile of v1, /device:TPU:8, one launch (start us, length us, event | category | flops | bytes accessed | tf_op | source)
XLA Modules:
  0.0 301.8 jit_solution(1745608261101848034)
XLA Ops:
  7.2 0.0 copy-start
  7.2 0.0 all-reduce.5.cloned.1.call-start
  7.2 1.0 convert_reduce_fusion
  8.2 0.7 compare_and_fusion
  8.9 0.1 select_reduce_fusion
  9.0 0.1 fusion.3
  9.1 1.5 bitcast_convert_fusion
  10.6 0.0 copy-done
  10.6 8.0 %gather_fusion = bf16[128,2,4096]{2,1,0:T(2,128)(2,1)} fusion(bf16[112,2,4096]{2,1,0:T(2,128)(2,1)S(1)} %bitcast.10, s32[1024]{0:T(1024)S(1)} %pad_clamp_fusion.1), kind=kCustom, calls=%fused_computation | custom fusion | bytes 4194816 | tf_op jit(solution)/shard_map/jit(_take)/gather | solution.py:46
  18.6 5.7 %fusion = f32[128,2,4096]{2,1,0:T(2,128)} fusion(pred[128]{0:T(512)(128)(4,1)S(1)} %fusion.3, bf16[128,2,4096]{2,1,0:T(2,128)(2,1)} %gather_fusion, pred[128]{0:T(512)(128)(4,1)S(1)} %compare_and_fusion.1), kind=kLoop, calls=%fused_computation.5 | loop fusion | flops 3145728 | bytes 6291712 | tf_op jit(solution)/shard_map/convert_element_type | solution.py:49
  24.4 0.0 all-reduce.5.cloned.1.call-update
  24.4 0.1 dynamic_slice.3
  24.5 1.3 dynamic-slice
  26.4 173.6 %all-reduce.5.cloned.1.call-done = (f32[128,2,4096]{2,1,0:T(2,128)}, f32[64,512]{1,0:T(8,128)}) async-done(((f32[128,2,4096]{2,1,0:T(2,128)}, f32[64,512]{1,0:T(8,128)}), (f32[128,2,4096]{2,1,0:T(2,128)}, f32[64,512]{1,0:T(8,128)})) %all-reduce.5.cloned.1.call-update) | async-done | bytes 4325392
  200.1 0.0 copy-done.6
  200.1 1.9 multiply_reduce_fusion
  202.0 12.4 %all-reduce.2 = (f32[2]{0:T(128)S(1)}, f32[2]{0:T(128)S(1)}) all-reduce(f32[2]{0:T(128)S(1)} %get-tuple-element.18, f32[2]{0:T(128)S(1)} %get-tuple-element.22), channel_id=1, replica_groups=mesh['dp'=64,'own'=8] {'own'}, use_global_device_ids=true, to_apply=%region_7.8 | all-reduce | flops 4 | bytes 32 | tf_op jit(solution)/shard_map/psum | solution.py:57
  214.4 0.8 fusion.7
  215.1 3.4 %stack.2 = bf16[64,2,2,4096]{3,2,1,0:T(2,128)(2,1)} broadcast(bf16[2,2,4096]{2,1,0:T(2,128)(2,1)S(1)} %get-tuple-element.16), dimensions={1,2,3} | broadcast | bytes 2129920 | tf_op jit(solution)/shard_map/stack | solution.py:66
  218.5 9.4 %all-to-all-start = ((bf16[64,2,2,4096]{3,2,1,0:T(2,128)(2,1)}), bf16[64,2,2,4096]{3,2,1,0:T(2,128)(2,1)}, u32[]{:S(2)}, u32[]{:S(2)}) async-start(bf16[64,2,2,4096]{3,2,1,0:T(2,128)(2,1)} %stack.2), calls=%async_computation | async-start | bytes 4194304 | tf_op jit(solution)/shard_map/all_to_all | solution.py:65
  228.0 0.8 divide_subtract_fusion
  228.8 52.1 %all-to-all-done = bf16[64,2,2,4096]{3,2,1,0:T(2,128)(2,1)} async-done(((bf16[64,2,2,4096]{3,2,1,0:T(2,128)(2,1)}), bf16[64,2,2,4096]{3,2,1,0:T(2,128)(2,1)}, u32[]{:S(2)}, u32[]{:S(2)}) %all-to-all-start) | async-done | bytes 2097184 | tf_op jit(solution)/shard_map/all_to_all | solution.py:65
  280.9 9.5 %gather_fusion.1 = bf16[112,2,4096]{2,1,0:T(2,128)(2,1)} fusion(bf16[128,2,4096]{2,1,0:T(2,128)(2,1)} %bitcast.4, s32[1024]{0:T(1024)S(1)} %pad_clamp_fusion), kind=kCustom, calls=%fused_computation.1 | custom fusion | bytes 3670464 | tf_op jit(solution)/shard_map/jit(_take)/gather | solution.py:72
  290.4 4.5 %broadcast_select_fusion.2 = bf16[112,2,4096]{2,1,0:T(2,128)(2,1)} fusion(bf16[112,2,4096]{2,1,0:T(2,128)(2,1)} %gather_fusion.1, pred[112]{0:T(512)(128)(4,1)S(1)} %get-tuple-element.14), kind=kLoop, calls=%fused_computation.4 | loop fusion | flops 917504 | bytes 3670128 | tf_op jit(solution)/shard_map/jit(_take)/select_n | solution.py:72
  (19 shorter events, 0.1 us)
Async XLA Ops:
  7.2 3.5 %copy-start = (bf16[1,112,2,4096]{3,2,1,0:T(2,128)(2,1)S(1)}, bf16[1,112,2,4096]{3,2,1,0:T(2,128)(2,1)}, u32[]{:S(2)}) copy-start(bf16[1,112,2,4096]{3,2,1,0:T(2,128)(2,1)} %param.9) | copy-start | bytes 5505028
  7.2 192.9 %all-reduce.5.cloned.1.call-start = ((), (), s32[]{:S(2)}) async-start(), calls=%async_computation.1 | async-start | bytes 8650752
  24.4 175.7 %copy-start.1 = (f32[2,2,4096]{2,1,0:T(2,128)S(1)}, f32[2,2,4096]{2,1,0:T(2,128)}, u32[]{:S(2)}) copy-start(f32[2,2,4096]{2,1,0:T(2,128)} %param.11) | copy-start | bytes 196612
  24.4 175.7 %copy-start.6 = (f32[2,2,4096]{2,1,0:T(2,128)S(1)}, f32[2,2,4096]{2,1,0:T(2,128)}, u32[]{:S(2)}) copy-start(f32[2,2,4096]{2,1,0:T(2,128)} %param.13) | copy-start | bytes 196612
  24.4 175.7 %copy-start.7 = (f32[2,2,4096]{2,1,0:T(2,128)S(1)}, f32[2,2,4096]{2,1,0:T(2,128)}, u32[]{:S(2)}) copy-start(f32[2,2,4096]{2,1,0:T(2,128)} %param.12) | copy-start | bytes 196612
  218.5 9.5 %copy-start.2 = (f32[64,512]{1,0:T(8,128)S(1)}, f32[64,512]{1,0:T(8,128)}, u32[]{:S(2)}) copy-start(f32[64,512]{1,0:T(8,128)} %param.15) | copy-start | bytes 393220
  218.5 9.5 %copy-start.3 = (f32[64,512]{1,0:T(8,128)S(1)}, f32[64,512]{1,0:T(8,128)}, u32[]{:S(2)}) copy-start(f32[64,512]{1,0:T(8,128)} %param.16) | copy-start | bytes 393220
  218.5 9.5 %copy-start.4 = (f32[64,512]{1,0:T(8,128)S(1)}, f32[64,512]{1,0:T(8,128)}, u32[]{:S(2)}) copy-start(f32[64,512]{1,0:T(8,128)} %param.17) | copy-start | bytes 393220
  218.5 9.5 %copy-start.5 = (f32[64,512]{1,0:T(8,128)S(1)}, f32[64,512]{1,0:T(8,128)}, u32[]{:S(2)}) copy-start(f32[64,512]{1,0:T(8,128)} %get-tuple-element.8) | copy-start | bytes 393220
  218.5 62.4 %all-to-all-start = ((bf16[64,2,2,4096]{3,2,1,0:T(2,128)(2,1)}), bf16[64,2,2,4096]{3,2,1,0:T(2,128)(2,1)}, u32[]{:S(2)}, u32[]{:S(2)}) async-start(bf16[64,2,2,4096]{3,2,1,0:T(2,128)(2,1)} %stack.2), calls=%async_computation | async-start | bytes 4194304 | tf_op jit(solution)/shard_map/all_to_all | solution.py:65
Sparse Core Ops, SparseCore 0:
  24.5 175.4 all-reduce.4
